TPU v7x, 32 devices: a whole 2x2x4 slice. The times are simulated.
32 devices in a mesh: dp: 2 (over x), space: 16 (over z, y, core).
Axes of the slice: x: 2, y: 2, z: 4, core: 2. Of those that a mesh axis runs over, the one named last changes fastest.
Arguments:
- stash: bfloat16 [16, 16, 4, 8640], P('space', None, 'dp'), may hold values from -5 to 5
- piece_map: int32 [16, 16], P(None, 'space'), may hold values from 0 to 15, as said below
- gain_one: float32 [768], replicated, may hold values from 0.5 to 1.5
- spec_one: float32 [2, 8, 96, 96], replicated, may hold values from -0.4375 to 0.4375
- bias_one: float32 [2, 768], replicated, may hold values from -3 to 3
- spec_two: float32 [2, 8, 96, 96], replicated, may hold values from -0.4375 to 0.4375
- bias_two: float32 [2, 768], replicated, may hold values from -0.6 to 0.6
- gain_two: float32 [768], replicated, may hold values from 0.5 to 1.5
- fc_one: bfloat16 [768, 3072], replicated, may hold values from -0.21875 to 0.21875
- bias_fc: float32 [3072], replicated, may hold values from -3 to 3
- fc_two: bfloat16 [3072, 768], replicated, may hold values from -0.109375 to 0.109375
- cotangent: bfloat16 [4, 16, 180, 768], P('dp', 'space'), may hold values from -6 to 6
Outputs:
- grad_input: float32 [4, 16, 180, 768], P('dp', 'space')
- grad_fc_one: float32 [768, 3072], P(None, ('dp', 'space'))
- grad_fc_two: float32 [3072, 768], P(('dp', 'space'))
- grad_bias_fc: float32 [3072], replicated
- grad_bias_out: float32 [768], replicated
- grad_gain_one: float32 [768], replicated
- grad_gain_two: float32 [768], replicated
- grad_spec_one: float32 [2, 8, 96, 96], replicated
- grad_bias_one: float32 [2, 768], replicated
- grad_spec_two: float32 [2, 8, 96, 96], replicated
- grad_bias_two: float32 [2, 768], replicated
Inputs may be any that keep to these rules, and one draw needn't show every extreme that they name: `piece_map`: each column holds every number from 0 to 15 once.
All inputs are finite; a program needn't handle non-finite values.
Results may differ from a plain program's by a relative error of at most 0.0046.
Values may be sent and summed in bfloat16 or wider, within the bound.
A program may use at most 128 MiB of HBM per device.

v0:
```python
import math
import jax
import jax.numpy as jnp
import numpy as np
from jax import lax
from jax.sharding import PartitionSpec as P

KW = 64
epsilon = 1e-05
high = lax.Precision.HIGH
everyone = ("dp", "space")


def layer_norm(values, gain_vector):
    centred = values - jnp.mean(values, axis=-1, keepdims=True)
    spread = jnp.mean(centred * centred, axis=-1, keepdims=True)
    return centred * lax.rsqrt(spread + epsilon) * gain_vector


def smooth_gate(values):
    return jax.nn.gelu(values, approximate=True)


def complex_blocks(weights):
    top = jnp.concatenate((weights[0], weights[1]), axis=2)
    bottom = jnp.concatenate((-weights[1], weights[0]), axis=2)
    return jnp.concatenate((top, bottom), axis=1)


def complex_bias(biases, blocks):
    return biases.reshape(2, blocks, 1, -1).transpose(1, 2, 0, 3).reshape(blocks, 1, -1)


def block_dot(values, weights):
    return jnp.einsum("nri,nio->nro", values, weights, precision=high)


def spectral_mlp(spectrum, spec_one, bias_one, spec_two, bias_two):
    blocks = spec_one.shape[1]
    inner = block_dot(spectrum, complex_blocks(spec_one)) + complex_bias(bias_one, blocks)
    return block_dot(smooth_gate(inner), complex_blocks(spec_two)) + complex_bias(bias_two, blocks)


def zonal_tables(length, ranks):
    positions = np.arange(length)[:, None]
    frequency = np.arange(KW)[None, :]
    angles = positions * frequency % length * (2.0 * math.pi / length)
    table = np.stack((np.cos(angles), -np.sin(angles))) / math.sqrt(length)
    doubled = table * np.where(frequency == 0, 1.0, 2.0)
    shaped = [
        item.reshape(2, length, ranks, KW // ranks).transpose(1, 2, 0, 3).astype(np.float32)
        for item in (table, doubled)
    ]
    return shaped


def meridian_table(length, ranks):
    positions = np.arange(length)
    angles = positions[:, None] * positions[None, :] % length * (2.0 * math.pi / length)
    cosine = np.cos(angles) / math.sqrt(length)
    sine = np.sin(angles) / math.sqrt(length)
    table = np.stack((np.stack((cosine, -sine), -1), np.stack((sine, cosine), -1)), 1)
    return table.reshape(ranks, length // ranks, 2, length, 2).astype(np.float32)


def swap(pieces):
    return lax.all_to_all(pieces, "space", split_axis=0, concat_axis=0, tiled=True)


def to_modes(field, zonal, merid, blocks, carried):
    pieces = jnp.einsum("brwd,wscm->sbrcmd", field, zonal, precision=high)
    modes = swap(pieces.astype(carried)).astype(jnp.float32)
    spectrum = jnp.einsum("lbrcmd,lrcke->bmked", modes, merid, precision=high)
    rows = math.prod(spectrum.shape[:3])
    split = spectrum.reshape(rows, 2, blocks, -1)
    return split.transpose(2, 0, 1, 3).reshape(blocks, rows, -1)


def from_modes(spectrum, zonal, merid, samples, width, carried):
    blocks, rows = spectrum.shape[:2]
    length = merid.shape[3]
    split = spectrum.reshape(blocks, rows, 2, -1).transpose(1, 2, 0, 3)
    shaped = split.reshape(samples, rows // (samples * length), length, 2, width)
    pieces = jnp.einsum("bmked,lrcke->lbrcmd", shaped, merid, precision=high)
    modes = swap(pieces.astype(carried)).astype(jnp.float32)
    return jnp.einsum("sbrcmd,wscm->brwd", modes, zonal, precision=high)


def local(
    stash,
    piece_map,
    gain_one,
    spec_one,
    bias_one,
    spec_two,
    bias_two,
    gain_two,
    fc_one,
    bias_fc,
    fc_two,
    cotangent,
):
    samples, lat_rows, lon_cells, model_width = cotangent.shape
    space_ranks = lax.axis_size("space")
    lat_total = lat_rows * space_ranks
    tokens = samples * lat_rows * lon_cells
    blocks = spec_one.shape[1]
    arrived = lax.all_to_all(stash, "space", split_axis=1, concat_axis=0, tiled=True)
    ordering = jnp.argsort(piece_map[:, 0])
    placed = jnp.take(arrived[:, 0], ordering, axis=0)
    inputs = jnp.transpose(placed, (1, 0, 2)).reshape(samples, lat_rows, lon_cells, model_width)
    base_field = inputs.astype(jnp.float32)
    zonal, zonal_back = zonal_tables(lon_cells, space_ranks)
    merid = meridian_table(lat_total, space_ranks)
    normed, pull_one = jax.vjp(layer_norm, base_field, gain_one)
    spectrum = to_modes(normed, zonal, merid, blocks, jnp.float32)
    mixed_spec, pull_mix = jax.vjp(spectral_mlp, spectrum, spec_one, bias_one, spec_two, bias_two)
    spatial = from_modes(mixed_spec, zonal_back, merid, samples, model_width, jnp.float32)
    mixed_field = base_field + normed + spatial
    normed_two, pull_two = jax.vjp(layer_norm, mixed_field, gain_two)
    normed_flat = normed_two.astype(jnp.bfloat16).reshape(tokens, model_width)
    hidden_pre = jnp.dot(normed_flat, fc_one, preferred_element_type=jnp.float32) + bias_fc
    active, pull_gate = jax.vjp(smooth_gate, hidden_pre)
    active_flat = active.astype(jnp.bfloat16)
    upstream = cotangent.reshape(tokens, model_width)
    term_two = jnp.einsum("tf,td->fd", active_flat, upstream, preferred_element_type=jnp.float32)
    part_two = lax.psum_scatter(
        term_two.astype(jnp.bfloat16), everyone, scatter_dimension=0, tiled=True
    )
    grad_active = jnp.einsum("td,fd->tf", upstream, fc_two, preferred_element_type=jnp.float32)
    grad_hidden = pull_gate(grad_active)[0]
    grad_hidden_flat = grad_hidden.astype(jnp.bfloat16)
    term_one = jnp.einsum(
        "tf,td->fd", grad_hidden_flat, normed_flat, preferred_element_type=jnp.float32
    )
    part_one = lax.psum_scatter(
        term_one.astype(jnp.bfloat16), everyone, scatter_dimension=0, tiled=True
    )
    grad_normed_two = jnp.einsum(
        "tf,df->td", grad_hidden_flat, fc_one, preferred_element_type=jnp.float32
    )
    grad_mixed_norm, grad_gain_two = pull_two(grad_normed_two.reshape(mixed_field.shape))
    grad_mixed = cotangent.astype(jnp.float32) + grad_mixed_norm
    grad_spectrum = to_modes(grad_mixed, zonal_back, merid, blocks, jnp.bfloat16)
    pulled = pull_mix(grad_spectrum)
    grad_normed = grad_mixed + from_modes(
        pulled[0], zonal, merid, samples, model_width, jnp.bfloat16
    )
    grad_base, grad_gain_one = pull_one(grad_normed)
    grad_input = grad_mixed + grad_base
    bias_sum = jnp.sum(grad_hidden, axis=0)
    out_sum = jnp.sum(cotangent, axis=(0, 1, 2), dtype=jnp.float32)
    totals = lax.psum(
        (
            grad_gain_one,
            grad_gain_two,
            pulled[1],
            pulled[2],
            pulled[3],
            pulled[4],
            bias_sum,
            out_sum,
        ),
        everyone,
    )
    grad_scale = 1.0 / math.sqrt(samples * lax.axis_size("dp") * lat_total * lon_cells)
    return (
        grad_input,
        (part_one.astype(jnp.float32) * grad_scale).T,
        part_two.astype(jnp.float32) * grad_scale,
        totals[6] * grad_scale,
        totals[7] * grad_scale,
        totals[0] * grad_scale,
        totals[1] * grad_scale,
        totals[2] * grad_scale,
        totals[3] * grad_scale,
        totals[4] * grad_scale,
        totals[5] * grad_scale,
    )


def solution(mesh):
    placed = (
        P("space", None, "dp", None),
        P(None, "space"),
        P(),
        P(),
        P(),
        P(),
        P(),
        P(),
        P(),
        P(),
        P(),
        P("dp", "space", None, None),
    )
    return jax.shard_map(
        local,
        mesh=mesh,
        in_specs=placed,
        out_specs=(
            P("dp", "space", None, None),
            P(None, ("dp", "space")),
            P(("dp", "space"), None),
            P(),
            P(),
            P(),
            P(),
            P(),
            P(),
            P(),
            P(),
        ),
        check_vma=False,
    )
```

profile of v0, /device:TPU:0, one launch (start us, length us, event | category | flops | bytes accessed | tf_op | source)
XLA Modules:
  0.0 514.6 jit_solution(12274644097293364253)
XLA Ops:
  7.2 7.4 %all-to-all-start = ((bf16[1,16,2,8640]{3,2,0,1:T(2,128)(2,1)}), bf16[1,16,2,8640]{3,2,0,1:T(2,128)(2,1)S(1)}, u32[]{:S(2)}, u32[]{:S(2)}) async-start(bf16[1,16,2,8640]{3,2,0,1:T(2,128)(2,1)} %bitcast.227), calls=%async_computation | async-start | bytes 1114112 | tf_op jit(solution)/shard_map/all_to_all | solution.py:108
  14.6 1.9 sort.17
  16.5 12.9 %all-to-all-done = bf16[1,16,2,8640]{3,2,0,1:T(2,128)(2,1)S(1)} async-done(((bf16[1,16,2,8640]{3,2,0,1:T(2,128)(2,1)}), bf16[1,16,2,8640]{3,2,0,1:T(2,128)(2,1)S(1)}, u32[]{:S(2)}, u32[]{:S(2)}) %all-to-all-start) | async-done | bytes 552992 | tf_op jit(solution)/shard_map/all_to_all | solution.py:108
  29.4 1.7 gather_fusion
  36.5 4.8 all-to-all-start.1
  42.8 1.9 fusion.71
  48.4 11.5 %all-to-all-done.1 = f32[16,2,1,2,4,768]{5,1,4,3,2,0:T(2,128)S(1)} async-done(((f32[16,2,1,2,4,768]{5,1,4,3,2,0:T(2,128)}), f32[16,2,1,2,4,768]{5,1,4,3,2,0:T(2,128)S(1)}, u32[]{:S(2)}, u32[]{:S(2)}) %all-to-all-start.1) | async-done | bytes 786464 | tf_op jit(solution)/shard_map/all_to_all | solution.py:67
  61.8 2.6 convolution_add_fusion.2
  68.9 5.6 %all-to-all-start.2 = ((f32[16,2,1,2,4,768]{5,4,1,3,2,0:T(4,128)}), f32[16,2,1,2,4,768]{5,4,1,3,2,0:T(4,128)}, u32[]{:S(2)}, u32[]{:S(2)}) async-start(f32[16,2,1,2,4,768]{5,4,1,3,2,0:T(4,128)} %copy.118), calls=%async_computation.2 | async-start | bytes 1572864 | tf_op jit(solution)/shard_map/all_to_all | solution.py:67
  75.3 6.7 %fusion.75 = f32[360,3072]{1,0:T(8,128)} fusion(bf16[360,768]{1,0:T(8,128)(2,1)S(1)} %reshape.326, bf16[3072,768]{1,0:T(8,128)(2,1)} %param.30), kind=kOutput, calls=%fused_computation.144 | convolution fusion | flops 1698693120 | bytes 9695232 | tf_op jit(solution)/shard_map/td,fd->tf/dot_general | solution.py:130
  81.9 11.3 %all-to-all-done.2 = f32[16,2,1,2,4,768]{5,4,1,3,2,0:T(4,128)} async-done(((f32[16,2,1,2,4,768]{5,4,1,3,2,0:T(4,128)}), f32[16,2,1,2,4,768]{5,4,1,3,2,0:T(4,128)}, u32[]{:S(2)}, u32[]{:S(2)}) %all-to-all-start.2) | async-done | bytes 786464 | tf_op jit(solution)/shard_map/all_to_all | solution.py:67
  93.2 2.4 fusion.73
  97.0 9.6 %fusion.68 = (f32[3072]{0:T(1024)S(1)}, bf16[360,3072]{1,0:T(8,128)(2,1)S(1)}, f32[360,3072]{1,0:T(8,128)}) fusion(f32[360,3072]{1,0:T(8,128)} %fusion.75, f32[3072]{0:T(1024)S(1)} %copy-done.27, bf16[360,768]{1,0:T(8,128)(2,1)S(1)} %reshape.337, bf16[768,3072]{1,0:T(8,128)(2,1)} %param.28), kind=kOutput, calls=%fused_computation.138 | convolution fusion | flops 1723020288 | bytes 16355328 | tf_op jit(solution)/shard_map/dot_general | solution.py:122
  108.1 5.2 %fusion.23 = f32[360,768]{1,0:T(8,128)} fusion(bf16[768,3072]{1,0:T(8,128)(2,1)} %param.28, bf16[360,3072]{1,0:T(8,128)(2,1)S(1)} %get-tuple-element.70), kind=kOutput, calls=%fused_computation.58 | convolution fusion | flops 1698693120 | bytes 8036352 | tf_op jit(solution)/shard_map/tf,df->td/dot_general | solution.py:139
  115.7 1.7 fusion.70
  118.3 17.5 %all_to_all.29 = bf16[16,2,1,2,4,768]{5,4,3,1,2,0:T(4,128)(2,1)S(1)} all-to-all(bf16[16,2,1,2,4,768]{5,4,3,1,2,0:T(4,128)(2,1)S(1)} %copy.120), channel_id=1, replica_groups=mesh['dp'=2,'space'=16] {'space'}, dimensions={0} | all-to-all | bytes 786432 | tf_op jit(solution)/shard_map/all_to_all | solution.py:67
  140.1 4.4 fusion.74
  149.7 6.5 %convolution_convert_fusion.1 = bf16[3072,768]{1,0:T(8,128)(2,1)} fusion(bf16[360,768]{1,0:T(8,128)(2,1)} %copy-done.15, bf16[360,3072]{1,0:T(8,128)(2,1)} %copy-done.30), kind=kOutput, calls=%fused_computation.4 | convolution fusion | flops 1701052416 | bytes 7483392 | tf_op jit(solution)/shard_map/tf,td->fd/dot_general | solution.py:133
  156.5 7.6 %convolution_convert_fusion = bf16[3072,768]{1,0:T(8,128)(2,1)} fusion(bf16[360,768]{1,0:T(8,128)(2,1)} %copy-done.14, f32[360,3072]{1,0:T(8,128)} %get-tuple-element.89), kind=kOutput, calls=%fused_computation.3 | convolution fusion | flops 1711005696 | bytes 9695232 | tf_op jit(solution)/shard_map/tf,td->fd/dot_general | solution.py:126
  164.1 4.6 fusion.21
  168.7 2.4 copy.126
  171.1 2.5 reshape.345
  173.6 1.7 fusion.14
  176.3 4.2 all-to-all-start.4
  180.9 100.9 %all-reduce.12.cloned.1.call-done = (f32[2,8,96,96]{3,2,1,0:T(8,128)}, f32[2,8,96,96]{3,2,1,0:T(8,128)}) async-done(((f32[2,8,96,96]{3,2,1,0:T(8,128)}, f32[2,8,96,96]{3,2,1,0:T(8,128)}), (f32[2,8,96,96]{3,2,1,0:T(8,128)}, f32[2,8,96,96]{3,2,1,0:T(8,128)})) %all-reduce.12.cloned.1.call-update) | async-done | bytes 1179664 | tf_op jit(solution)/shard_map/psum | solution.py:153
  281.8 2.7 broadcast_multiply_fusion
  284.6 2.0 multiply_reduce_fusion.2
  287.7 2.1 copy.132
  289.8 39.8 %all-reduce.8 = (f32[3072]{0:T(1024)S(1)}, f32[768]{0:T(1024)S(1)}, f32[768]{0:T(1024)S(1)}, f32[768]{0:T(1024)S(1)}, f32[2,768]{1,0:T(2,128)S(1)}, /*index=5*/f32[2,768]{1,0:T(2,128)S(1)}) all-reduce(f32[3072]{0:T(1024)S(1)} %get-tuple-element.69, ...), channel_id=1, replica_groups=mesh['dp'=2,'space'=16] {'dp','space'}, use_global_device_ids=true, to_apply=%region_12.13 | all-reduce | flops 8448 | bytes 67584 | tf_op jit(solution)/shard_map/psum | solution.py:153
  332.0 62.0 %reduce-scatter.3.cloned.1.call-done = bf16[96,768]{1,0:T(8,128)(2,1)} async-done(((bf16[3072,768]{1,0:T(8,128)(2,1)}), bf16[96,768]{1,0:T(8,128)(2,1)}) %reduce-scatter.3.cloned.1.call-update) | async-done | bytes 147472 | tf_op jit(solution)/shard_map/reduce_scatter | solution.py:136
  394.0 1.6 multiply_bitcast_fusion
  395.7 110.6 %reduce-scatter.5.cloned.1.call-done = bf16[96,768]{1,0:T(8,128)(2,1)} async-done(((bf16[3072,768]{1,0:T(8,128)(2,1)}), bf16[96,768]{1,0:T(8,128)(2,1)}) %reduce-scatter.5.cloned.1.call-update) | async-done | bytes 147472 | tf_op jit(solution)/shard_map/reduce_scatter | solution.py:127
  (143 shorter events, 39.9 us)
Async XLA Ops:
  7.2 22.2 %all-to-all-start = ((bf16[1,16,2,8640]{3,2,0,1:T(2,128)(2,1)}), bf16[1,16,2,8640]{3,2,0,1:T(2,128)(2,1)S(1)}, u32[]{:S(2)}, u32[]{:S(2)}) async-start(bf16[1,16,2,8640]{3,2,0,1:T(2,128)(2,1)} %bitcast.227), calls=%async_computation | async-start | bytes 1114112 | tf_op jit(solution)/shard_map/all_to_all | solution.py:108
  36.5 4.8 copy-start.25
  36.5 5.0 copy-start.26
  36.5 5.1 copy-start.10
  36.5 23.4 %all-to-all-start.1 = ((f32[16,2,1,2,4,768]{5,1,4,3,2,0:T(2,128)}), f32[16,2,1,2,4,768]{5,1,4,3,2,0:T(2,128)S(1)}, u32[]{:S(2)}, u32[]{:S(2)}) async-start(f32[16,2,1,2,4,768]{5,1,4,3,2,0:T(2,128)} %copy.105), calls=%async_computation.1 | async-start | bytes 1572864 | tf_op jit(solution)/shard_map/all_to_all | solution.py:67
  41.8 19.9 %copy-start.7 = (f32[1,8,96,96]{2,3,1,0:T(8,128)}, f32[1,8,96,96]{2,3,1,0:T(8,128)S(1)}, u32[]{:S(2)}) copy-start(f32[1,8,96,96]{2,3,1,0:T(8,128)S(1)} %copy.159) | copy-start | bytes 884740
  45.9 2.5 copy-start.8
  45.9 14.0 %copy-start.20 = (f32[16,2,16,2,1,1]{0,2,1,3,5,4:T(8,128)S(1)}, f32[16,2,16,2,1,1]{0,2,1,3,5,4:T(8,128)}, u32[]{:S(2)}) copy-start(f32[16,2,16,2,1,1]{0,2,1,3,5,4:T(8,128)} %constant.86) | copy-start | bytes 12292
  61.8 2.6 copy-start.4
  61.8 2.6 copy-start.9
  61.8 2.6 copy-start.16
  61.8 2.6 copy-start.17
  64.4 1.4 copy-start.11
  68.9 6.2 %copy-start.1 = (bf16[2,1,180,768]{3,0,2,1:T(2,128)(2,1)S(1)}, bf16[2,1,180,768]{3,0,2,1:T(2,128)(2,1)}, u32[]{:S(2)}) copy-start(bf16[2,1,180,768]{3,0,2,1:T(2,128)(2,1)} %param.31) | copy-start | bytes 1658884
  68.9 24.3 %all-to-all-start.2 = ((f32[16,2,1,2,4,768]{5,4,1,3,2,0:T(4,128)}), f32[16,2,1,2,4,768]{5,4,1,3,2,0:T(4,128)}, u32[]{:S(2)}, u32[]{:S(2)}) async-start(f32[16,2,1,2,4,768]{5,4,1,3,2,0:T(4,128)} %copy.118), calls=%async_computation.2 | async-start | bytes 1572864 | tf_op jit(solution)/shard_map/all_to_all | solution.py:67
  74.5 207.4 %all-reduce.12.cloned.1.call-start = ((), (), s32[]{:S(2)}) async-start(), calls=%async_computation.9 | async-start | bytes 3145728 | tf_op jit(solution)/shard_map/psum | solution.py:153
  75.2 6.7 %copy-start.14 = (bf16[360,768]{1,0:T(8,128)(2,1)}, bf16[360,768]{1,0:T(8,128)(2,1)S(1)}, u32[]{:S(2)}) copy-start(bf16[360,768]{1,0:T(8,128)(2,1)S(1)} %reshape.326) | copy-start | bytes 1658884
  75.3 18.0 %copy-start.29 = (f32[180,16,2,4,1]{0,1,3,4,2:T(8,128)S(1)}, f32[180,16,2,4,1]{0,1,3,4,2:T(8,128)}, u32[]{:S(2)}) copy-start(f32[180,16,2,4,1]{0,1,3,4,2:T(8,128)} %constant.85) | copy-start | bytes 276484
  97.0 9.6 %copy-start.15 = (bf16[360,768]{1,0:T(8,128)(2,1)}, bf16[360,768]{1,0:T(8,128)(2,1)S(1)}, u32[]{:S(2)}) copy-start(bf16[360,768]{1,0:T(8,128)(2,1)S(1)} %reshape.337) | copy-start | bytes 1658884
  106.6 1.4 copy-start.30
  115.7 1.8 copy-start.2
  115.7 1.8 copy-start.18
  140.1 4.4 copy-start.6
  140.1 4.4 copy-start.12
  144.5 1.2 copy-start.13
  145.4 1.1 copy-start.5
  149.7 244.3 %reduce-scatter.3.cloned.1.call-start = ((), (), s32[]{:S(2)}) async-start(), calls=%async_computation.7 | async-start | bytes 4866048 | tf_op jit(solution)/shard_map/reduce_scatter | solution.py:136
  156.3 350.0 %reduce-scatter.5.cloned.1.call-start = ((), (), s32[]{:S(2)}) async-start(), calls=%async_computation.8 | async-start | bytes 4866048 | tf_op jit(solution)/shard_map/reduce_scatter | solution.py:127
  171.1 2.5 copy-start.23
  176.3 108.3 %all-to-all-start.4 = ((bf16[16,2,1,2,4,768]{5,3,4,1,2,0:T(2,128)(2,1)}), bf16[16,2,1,2,4,768]{5,3,4,1,2,0:T(2,128)(2,1)}, u32[]{:S(2)}, u32[]{:S(2)}) async-start(bf16[16,2,1,2,4,768]{5,3,4,1,2,0:T(2,128)(2,1)} %copy.129), calls=%async_computation.4 | async-start | bytes 786432 | tf_op jit(solution)/shard_map/all_to_all | solution.py:67
  281.8 2.7 copy-start.3
  281.8 2.7 copy-start.28
  (6 other events, 5.0 us)
Sparse Core Ops, SparseCore 0:
  149.8 131.9 all-reduce.11
  287.3 106.6 reduce-scatter.2
  399.5 106.6 reduce-scatter.4
where the time goes:
time: 521 us; the launch traced here: 515 us
  waiting for transfers between devices  309 us (59%)
  matrix products  59.3 us (11%)
  blocking collectives  57.3 us (11%)
  local copies, waits for them, and re-layouts  31.9 us (6%)
  starting transfers between devices  22.8 us (4%)
  other arithmetic  19.5 us (4%)
  between operations  14.6 us (3%)
    reduce_scatter x1, waiting for transfers between devices, local(): lax.psum_scatter(term_two.astype(jnp.bfloat16), everyone, scatter_dimensi...  111 us
    psum x1, waiting for transfers between devices, local(): lax.psum((grad_gain_one, grad_gain_two, pulled[1], pulled[2], pulled[3],...  101 us
    reduce_scatter x1, waiting for transfers between devices, local(): lax.psum_scatter(term_one.astype(jnp.bfloat16), everyone, scatter_dimensi...  62 us
    psum x1, blocking collectives, local(): lax.psum((grad_gain_one, grad_gain_two, pulled[1], pulled[2], pulled[3],...  39.8 us
    all_to_all x3, waiting for transfers between devices, swap(): lax.all_to_all(pieces, 'space', split_axis=0, concat_axis=0, tiled=True)  22.8 us
    all_to_all x1, blocking collectives, swap(): lax.all_to_all(pieces, 'space', split_axis=0, concat_axis=0, tiled=True)  17.5 us
    dot_general x6, matrix products, block_dot(): return jnp.einsum('nri,nio->nro', values, weights, precision=high)  14.6 us
    all_to_all x3, starting transfers between devices, swap(): lax.all_to_all(pieces, 'space', split_axis=0, concat_axis=0, tiled=True)  14.5 us
  transfers between devices with their start and end apart: 7, of which 6 were waited for; matrix products, arithmetic and copies ran while one was open for 11% of the time, Pallas kernels for 0%

commit v1 on v0

--- a/solution.py
+++ b/solution.py
@@ -151,17 +151,20 @@
     bias_sum = jnp.sum(grad_hidden, axis=0)
     out_sum = jnp.sum(cotangent, axis=(0, 1, 2), dtype=jnp.float32)
     totals = lax.psum(
-        (
-            grad_gain_one,
-            grad_gain_two,
-            pulled[1],
-            pulled[2],
-            pulled[3],
-            pulled[4],
-            bias_sum,
-            out_sum,
+        lax.psum(
+            (
+                grad_gain_one,
+                grad_gain_two,
+                pulled[1],
+                pulled[2],
+                pulled[3],
+                pulled[4],
+                bias_sum,
+                out_sum,
+            ),
+            "space",
         ),
-        everyone,
+        "dp",
     )
     grad_scale = 1.0 / math.sqrt(samples * lax.axis_size("dp") * lat_total * lon_cells)
     return (

time: 521 us -> 486 us (0.933)
  waiting for transfers between devices: 309 us -> 243 us
  blocking collectives: 57.3 us -> 86.5 us
    reduce_scatter x1, waiting for transfers between devices: 62 us -> 0.01 us  [local(): lax.psum_scatter(term_one.astype(jnp.bfloat16), everyone, scatter_dimensi...]
    psum x1, blocking collectives: 39.8 us -> 60.5 us  [local(): lax.psum((grad_gain_one, grad_gain_two, pulled[1], pulled[2], pulled[3],...]
    all_to_all x3, waiting for transfers between devices: 22.8 us -> 34.6 us  [swap(): lax.all_to_all(pieces, 'space', split_axis=0, concat_axis=0, tiled=True)]
    reduce_scatter x1, waiting for transfers between devices: 111 us -> 100 us  [local(): lax.psum_scatter(term_two.astype(jnp.bfloat16), everyone, scatter_dimensi...]
    psum x0 -> x1, blocking collectives: none -> 8.47 us  [local(): lax.psum(lax.psum((grad_gain_one, grad_gain_two, pulled[1], pulled[2], pu...]
    psum x1, waiting for transfers between devices: 101 us -> 95 us  [local(): lax.psum((grad_gain_one, grad_gain_two, pulled[1], pulled[2], pulled[3],...]
  transfers between devices with their start and end apart: 7 -> 8, of which waited for: 6 -> 6; matrix products, arithmetic and copies ran while one was open for 11% -> 11% of each run, Pallas kernels for 0% -> 0%
where the time goes in v1:
time: 486 us; the launch traced here: 480 us
  waiting for transfers between devices  243 us (50%)
  blocking collectives  86.5 us (18%)
  matrix products  59.6 us (12%)
  local copies, waits for them, and re-layouts  32.4 us (7%)
  starting transfers between devices  22.9 us (5%)
  other arithmetic  19.3 us (4%)
  between operations  16.3 us (3%)
    reduce_scatter x1, waiting for transfers between devices, local(): lax.psum_scatter(term_two.astype(jnp.bfloat16), everyone, scatter_dimensi...  100 us
    psum x1, waiting for transfers between devices, local(): lax.psum((grad_gain_one, grad_gain_two, pulled[1], pulled[2], pulled[3],...  95 us
    psum x1, blocking collectives, local(): lax.psum((grad_gain_one, grad_gain_two, pulled[1], pulled[2], pulled[3],...  60.5 us
    all_to_all x3, waiting for transfers between devices, swap(): lax.all_to_all(pieces, 'space', split_axis=0, concat_axis=0, tiled=True)  34.6 us
    all_to_all x1, blocking collectives, swap(): lax.all_to_all(pieces, 'space', split_axis=0, concat_axis=0, tiled=True)  17.5 us
    dot_general x6, matrix products, block_dot(): return jnp.einsum('nri,nio->nro', values, weights, precision=high)  14.7 us
    all_to_all x3, starting transfers between devices, swap(): lax.all_to_all(pieces, 'space', split_axis=0, concat_axis=0, tiled=True)  14.6 us
    all_to_all x1, waiting for transfers between devices, local(): lax.all_to_all(stash, 'space', split_axis=1, concat_axis=0, tiled=True)  12.9 us
  transfers between devices with their start and end apart: 8, of which 6 were waited for; matrix products, arithmetic and copies ran while one was open for 11% of the time, Pallas kernels for 0%

profile of v1, /device:TPU:0, one launch (start us, length us, event | category | flops | bytes accessed | tf_op | source)
XLA Modules:
  0.0 480.0 jit_solution(2045607528156852707)
XLA Ops:
  8.0 7.4 %all-to-all-start = ((bf16[1,16,2,8640]{3,2,0,1:T(2,128)(2,1)}), bf16[1,16,2,8640]{3,2,0,1:T(2,128)(2,1)S(1)}, u32[]{:S(2)}, u32[]{:S(2)}) async-start(bf16[1,16,2,8640]{3,2,0,1:T(2,128)(2,1)} %bitcast.227), calls=%async_computation | async-start | bytes 1114112 | tf_op jit(solution)/shard_map/all_to_all | solution.py:108
  15.5 1.9 sort.17
  17.4 12.9 %all-to-all-done = bf16[1,16,2,8640]{3,2,0,1:T(2,128)(2,1)S(1)} async-done(((bf16[1,16,2,8640]{3,2,0,1:T(2,128)(2,1)}), bf16[1,16,2,8640]{3,2,0,1:T(2,128)(2,1)S(1)}, u32[]{:S(2)}, u32[]{:S(2)}) %all-to-all-start) | async-done | bytes 552992 | tf_op jit(solution)/shard_map/all_to_all | solution.py:108
  30.2 1.7 gather_fusion
  37.3 4.8 all-to-all-start.1
  43.6 1.9 fusion.71
  49.2 11.5 %all-to-all-done.1 = f32[16,2,1,2,4,768]{5,1,4,3,2,0:T(2,128)S(1)} async-done(((f32[16,2,1,2,4,768]{5,1,4,3,2,0:T(2,128)}), f32[16,2,1,2,4,768]{5,1,4,3,2,0:T(2,128)S(1)}, u32[]{:S(2)}, u32[]{:S(2)}) %all-to-all-start.1) | async-done | bytes 786464 | tf_op jit(solution)/shard_map/all_to_all | solution.py:67
  62.7 2.6 convolution_add_fusion.2
  69.8 5.6 %all-to-all-start.2 = ((f32[16,2,1,2,4,768]{5,4,1,3,2,0:T(4,128)}), f32[16,2,1,2,4,768]{5,4,1,3,2,0:T(4,128)}, u32[]{:S(2)}, u32[]{:S(2)}) async-start(f32[16,2,1,2,4,768]{5,4,1,3,2,0:T(4,128)} %copy.118), calls=%async_computation.2 | async-start | bytes 1572864 | tf_op jit(solution)/shard_map/all_to_all | solution.py:67
  76.1 6.7 %fusion.75 = f32[360,3072]{1,0:T(8,128)} fusion(bf16[360,768]{1,0:T(8,128)(2,1)S(1)} %reshape.326, bf16[3072,768]{1,0:T(8,128)(2,1)} %param.30), kind=kOutput, calls=%fused_computation.144 | convolution fusion | flops 1698693120 | bytes 9695232 | tf_op jit(solution)/shard_map/td,fd->tf/dot_general | solution.py:130
  82.8 11.3 %all-to-all-done.2 = f32[16,2,1,2,4,768]{5,4,1,3,2,0:T(4,128)} async-done(((f32[16,2,1,2,4,768]{5,4,1,3,2,0:T(4,128)}), f32[16,2,1,2,4,768]{5,4,1,3,2,0:T(4,128)}, u32[]{:S(2)}, u32[]{:S(2)}) %all-to-all-start.2) | async-done | bytes 786464 | tf_op jit(solution)/shard_map/all_to_all | solution.py:67
  94.1 2.4 fusion.73
  97.8 9.6 %fusion.68 = (f32[3072]{0:T(1024)S(1)}, bf16[360,3072]{1,0:T(8,128)(2,1)S(1)}, f32[360,3072]{1,0:T(8,128)}) fusion(f32[360,3072]{1,0:T(8,128)} %fusion.75, f32[3072]{0:T(1024)S(1)} %copy-done.28, bf16[360,768]{1,0:T(8,128)(2,1)S(1)} %reshape.337, bf16[768,3072]{1,0:T(8,128)(2,1)} %param.28), kind=kOutput, calls=%fused_computation.138 | convolution fusion | flops 1723020288 | bytes 16355328 | tf_op jit(solution)/shard_map/dot_general | solution.py:122
  108.9 5.2 %fusion.23 = f32[360,768]{1,0:T(8,128)} fusion(bf16[768,3072]{1,0:T(8,128)(2,1)} %param.28, bf16[360,3072]{1,0:T(8,128)(2,1)S(1)} %get-tuple-element.78), kind=kOutput, calls=%fused_computation.58 | convolution fusion | flops 1698693120 | bytes 8036352 | tf_op jit(solution)/shard_map/tf,df->td/dot_general | solution.py:139
  116.5 1.7 fusion.70
  119.2 17.5 %all_to_all.29 = bf16[16,2,1,2,4,768]{5,4,3,1,2,0:T(4,128)(2,1)S(1)} all-to-all(bf16[16,2,1,2,4,768]{5,4,3,1,2,0:T(4,128)(2,1)S(1)} %copy.120), channel_id=1, replica_groups=mesh['dp'=2,'space'=16] {'space'}, dimensions={0} | all-to-all | bytes 786432 | tf_op jit(solution)/shard_map/all_to_all | solution.py:67
  140.9 4.4 fusion.74
  150.0 95.0 %all-reduce.15.cloned.1.call-done = (f32[2,8,96,96]{3,2,1,0:T(8,128)}, f32[2,8,96,96]{3,2,1,0:T(8,128)}) async-done(((f32[2,8,96,96]{3,2,1,0:T(8,128)}, f32[2,8,96,96]{3,2,1,0:T(8,128)}), (f32[2,8,96,96]{3,2,1,0:T(8,128)}, f32[2,8,96,96]{3,2,1,0:T(8,128)})) %all-reduce.15.cloned.1.call-update) | async-done | bytes 1179664 | tf_op jit(solution)/shard_map/psum | solution.py:154
  245.0 6.5 %convolution_convert_fusion.1 = bf16[3072,768]{1,0:T(8,128)(2,1)} fusion(bf16[360,768]{1,0:T(8,128)(2,1)} %copy-done.16, bf16[360,3072]{1,0:T(8,128)(2,1)} %copy-done.30), kind=kOutput, calls=%fused_computation.4 | convolution fusion | flops 1701052416 | bytes 7483392 | tf_op jit(solution)/shard_map/tf,td->fd/dot_general | solution.py:133
  251.9 7.6 %convolution_convert_fusion = bf16[3072,768]{1,0:T(8,128)(2,1)} fusion(bf16[360,768]{1,0:T(8,128)(2,1)} %copy-done.15, f32[360,3072]{1,0:T(8,128)} %get-tuple-element.97), kind=kOutput, calls=%fused_computation.3 | convolution fusion | flops 1711005696 | bytes 9695232 | tf_op jit(solution)/shard_map/tf,td->fd/dot_general | solution.py:126
  259.4 4.6 fusion.21
  264.1 2.5 copy.126
  266.5 2.5 reshape.345
  269.0 1.7 fusion.14
  271.7 4.3 all-to-all-start.4
  276.4 11.8 %all-to-all-done.4 = bf16[16,2,1,2,4,768]{5,3,4,1,2,0:T(2,128)(2,1)} async-done(((bf16[16,2,1,2,4,768]{5,3,4,1,2,0:T(2,128)(2,1)}), bf16[16,2,1,2,4,768]{5,3,4,1,2,0:T(2,128)(2,1)}, u32[]{:S(2)}, u32[]{:S(2)}) %all-to-all-start.4) | async-done | bytes 393248 | tf_op jit(solution)/shard_map/all_to_all | solution.py:67
  288.2 2.2 multiply_reduce_fusion.2
  292.1 2.1 copy.132
  294.2 60.5 %all-reduce.8 = (f32[3072]{0:T(1024)S(1)}, f32[768]{0:T(1024)S(1)}, f32[768]{0:T(1024)S(1)}, f32[768]{0:T(1024)S(1)}, f32[2,768]{1,0:T(2,128)S(1)}, /*index=5*/f32[2,768]{1,0:T(2,128)S(1)}) all-reduce(f32[3072]{0:T(1024)S(1)} %get-tuple-element.77, f32[768]{0:T(1024)S(1)} %get-tuple-element.93, ...), channel_id=1, replica_groups=mesh['dp'=2,'space'=16] {'space'}, use_global_device_ids=true, to_apply=%region_12.13 | all-reduce | flops 8448 | bytes 67584 | tf_op jit(solution)/shard_map/psum | solution.py:154
  354.7 8.5 %all-reduce.10 = (f32[3072]{0:T(1024)S(1)}, f32[768]{0:T(1024)S(1)}, f32[768]{0:T(1024)S(1)}, f32[768]{0:T(1024)S(1)}, f32[2,768]{1,0:T(2,128)S(1)}, /*index=5*/f32[2,768]{1,0:T(2,128)S(1)}) all-reduce(f32[3072]{0:T(1024)S(1)} %get-tuple-element.61, f32[768]{0:T(1024)S(1)} %get-tuple-element.62, ...), channel_id=1, replica_groups=mesh['dp'=2,'space'=16] {'dp'}, use_global_device_ids=true, to_apply=%region_13.14 | all-reduce | flops 8448 | bytes 67584 | tf_op jit(solution)/shard_map/psum | solution.py:153
  365.6 2.2 broadcast_multiply_fusion.1
  370.4 100.3 %reduce-scatter.5.cloned.1.call-done = bf16[96,768]{1,0:T(8,128)(2,1)} async-done(((bf16[3072,768]{1,0:T(8,128)(2,1)}), bf16[96,768]{1,0:T(8,128)(2,1)}) %reduce-scatter.5.cloned.1.call-update) | async-done | bytes 147472 | tf_op jit(solution)/shard_map/reduce_scatter | solution.py:127
  (147 shorter events, 42.4 us)
Async XLA Ops:
  8.0 22.2 %all-to-all-start = ((bf16[1,16,2,8640]{3,2,0,1:T(2,128)(2,1)}), bf16[1,16,2,8640]{3,2,0,1:T(2,128)(2,1)S(1)}, u32[]{:S(2)}, u32[]{:S(2)}) async-start(bf16[1,16,2,8640]{3,2,0,1:T(2,128)(2,1)} %bitcast.227), calls=%async_computation | async-start | bytes 1114112 | tf_op jit(solution)/shard_map/all_to_all | solution.py:108
  37.3 4.8 copy-start.26
  37.3 5.0 %copy-start.27 = (f32[2,768]{1,0:T(2,128)S(1)}, f32[2,768]{1,0:T(2,128)}, u32[]{:S(2)}) copy-start(f32[2,768]{1,0:T(2,128)} %param.26) | copy-start | bytes 18436
  37.3 5.1 %copy-start.10 = (f32[2,8,96,96]{3,2,1,0:T(8,128)S(1)}, f32[2,8,96,96]{3,2,1,0:T(8,128)}, u32[]{:S(2)}) copy-start(f32[2,8,96,96]{3,2,1,0:T(8,128)} %param.23) | copy-start | bytes 1769476
  37.3 23.4 %all-to-all-start.1 = ((f32[16,2,1,2,4,768]{5,1,4,3,2,0:T(2,128)}), f32[16,2,1,2,4,768]{5,1,4,3,2,0:T(2,128)S(1)}, u32[]{:S(2)}, u32[]{:S(2)}) async-start(f32[16,2,1,2,4,768]{5,1,4,3,2,0:T(2,128)} %copy.105), calls=%async_computation.1 | async-start | bytes 1572864 | tf_op jit(solution)/shard_map/all_to_all | solution.py:67
  42.7 19.9 %copy-start.7 = (f32[1,8,96,96]{2,3,1,0:T(8,128)}, f32[1,8,96,96]{2,3,1,0:T(8,128)S(1)}, u32[]{:S(2)}) copy-start(f32[1,8,96,96]{2,3,1,0:T(8,128)S(1)} %copy.159) | copy-start | bytes 884740
  46.7 2.5 copy-start.8
  46.7 14.0 %copy-start.21 = (f32[16,2,16,2,1,1]{0,2,1,3,5,4:T(8,128)S(1)}, f32[16,2,16,2,1,1]{0,2,1,3,5,4:T(8,128)}, u32[]{:S(2)}) copy-start(f32[16,2,16,2,1,1]{0,2,1,3,5,4:T(8,128)} %constant.86) | copy-start | bytes 12292
  62.6 2.6 copy-start.4
  62.6 2.6 copy-start.9
  62.6 2.6 copy-start.17
  62.6 2.6 copy-start.18
  65.2 1.4 copy-start.13
  69.7 6.1 %copy-start.1 = (bf16[2,1,180,768]{3,0,2,1:T(2,128)(2,1)S(1)}, bf16[2,1,180,768]{3,0,2,1:T(2,128)(2,1)}, u32[]{:S(2)}) copy-start(bf16[2,1,180,768]{3,0,2,1:T(2,128)(2,1)} %param.31) | copy-start | bytes 1658884
  69.8 24.3 %all-to-all-start.2 = ((f32[16,2,1,2,4,768]{5,4,1,3,2,0:T(4,128)}), f32[16,2,1,2,4,768]{5,4,1,3,2,0:T(4,128)}, u32[]{:S(2)}, u32[]{:S(2)}) async-start(f32[16,2,1,2,4,768]{5,4,1,3,2,0:T(4,128)} %copy.118), calls=%async_computation.2 | async-start | bytes 1572864 | tf_op jit(solution)/shard_map/all_to_all | solution.py:67
  75.3 169.7 %all-reduce.15.cloned.1.call-start = ((), (), s32[]{:S(2)}) async-start(), calls=%async_computation.9 | async-start | bytes 3145728 | tf_op jit(solution)/shard_map/psum | solution.py:154
  76.1 6.7 %copy-start.15 = (bf16[360,768]{1,0:T(8,128)(2,1)}, bf16[360,768]{1,0:T(8,128)(2,1)S(1)}, u32[]{:S(2)}) copy-start(bf16[360,768]{1,0:T(8,128)(2,1)S(1)} %reshape.326) | copy-start | bytes 1658884
  76.1 18.0 %copy-start.29 = (f32[180,16,2,4,1]{0,1,3,4,2:T(8,128)S(1)}, f32[180,16,2,4,1]{0,1,3,4,2:T(8,128)}, u32[]{:S(2)}) copy-start(f32[180,16,2,4,1]{0,1,3,4,2:T(8,128)} %constant.85) | copy-start | bytes 276484
  97.8 9.6 %copy-start.16 = (bf16[360,768]{1,0:T(8,128)(2,1)}, bf16[360,768]{1,0:T(8,128)(2,1)S(1)}, u32[]{:S(2)}) copy-start(bf16[360,768]{1,0:T(8,128)(2,1)S(1)} %reshape.337) | copy-start | bytes 1658884
  107.5 1.4 copy-start.30
  116.5 1.8 copy-start.2
  116.5 1.8 copy-start.19
  140.9 4.4 copy-start.6
  140.9 4.4 copy-start.14
  145.3 1.2 copy-start.12
  146.2 1.1 copy-start.5
  149.9 215.7 %all-reduce.17.cloned.1.call-start = ((), (), s32[]{:S(2)}) async-start(), calls=%async_computation.10 | async-start | bytes 3145728 | tf_op jit(solution)/shard_map/psum | solution.py:153
  245.0 123.7 %reduce-scatter.3.cloned.1.call-start = ((), (), s32[]{:S(2)}) async-start(), calls=%async_computation.7 | async-start | bytes 4866048 | tf_op jit(solution)/shard_map/reduce_scatter | solution.py:136
  251.6 219.1 %reduce-scatter.5.cloned.1.call-start = ((), (), s32[]{:S(2)}) async-start(), calls=%async_computation.8 | async-start | bytes 4866048 | tf_op jit(solution)/shard_map/reduce_scatter | solution.py:127
  266.5 2.5 copy-start.24
  271.7 16.5 %all-to-all-start.4 = ((bf16[16,2,1,2,4,768]{5,3,4,1,2,0:T(2,128)(2,1)}), bf16[16,2,1,2,4,768]{5,3,4,1,2,0:T(2,128)(2,1)}, u32[]{:S(2)}, u32[]{:S(2)}) async-start(bf16[16,2,1,2,4,768]{5,3,4,1,2,0:T(2,128)(2,1)} %copy.129), calls=%async_computation.4 | async-start | bytes 786432 | tf_op jit(solution)/shard_map/all_to_all | solution.py:67
  365.6 2.2 copy-start.11
  (7 other events, 6.0 us)
Sparse Core Ops, SparseCore 0:
  150.0 94.8 all-reduce.14
  247.3 50.5 all-reduce.16
Sparse Core Ops, SparseCore 1:
  251.7 106.9 reduce-scatter.2
  364.0 106.7 reduce-scatter.4
